TPU v7x, 128 devices: a whole 4x4x4 slice. The times are simulated.
128 devices in a mesh: req: 16 (over z, x), mlp: 8 (over y, core).
Axes of the slice: x: 4, y: 4, z: 4, core: 2. Of those that a mesh axis runs over, the one named last changes fastest.
Arguments:
- tokens: bfloat16 [65536, 1024], P(('req', 'mlp')), may hold values from -72 to 72
- attend_weight: bfloat16 [1024, 3072], replicated, may hold values from -0.1875 to 0.1875
- output_weight: bfloat16 [1024, 1024], replicated, may hold values from -0.1875 to 0.1875
- attend_gain: float32 [1024], replicated, may hold values from 0.1 to 1.9
- up_weight: bfloat16 [1024, 4096], P(None, 'mlp'), may hold values from -0.1875 to 0.1875
- down_weight: bfloat16 [1024, 4096], P(None, 'mlp'), may hold values from -0.09375 to 0.09375
- mlp_gain: float32 [1024], replicated, may hold values from 0.1 to 1.9
- embed_weight: bfloat16 [1024, 128], replicated, may hold values from -0.1875 to 0.1875
- query_length: int32 [512], P(('req', 'mlp')), may hold values from 1 to 128, 49152 in all
- documents: bfloat16 [128, 256, 128], P('req', 'mlp'), may hold values from -0.54 to 0.54
- document_length: int32 [128], P('req'), may hold values from 1 to 256, 16512 in all
- candidates: int32 [512, 8], P(('req', 'mlp')), may hold values from 0 to 127
Outputs:
- embedded: bfloat16 [65536, 128], P(('req', 'mlp'))
- scores: float32 [512, 8], P(('req', 'mlp'))
All inputs are finite; a program needn't handle non-finite values. No bound on the sum of `query_length` or of `document_length` on one device may be relied on, other than what follows from the above.
Results may differ from a plain program's by a relative error of at most 0.015.
The roundings to bfloat16 on the way count: a program that leaves them out, or rounds other values in their place, can miss the bound.
Values may be sent and summed in bfloat16 or wider, within the bound.
No kernel may reach another device: no remote copies, remote signals or barrier semaphores. Data moves between devices by JAX's collectives and lax.ppermute only.
A program may use at most 128 MiB of HBM per device.

v0:
```python
import jax
import jax.numpy as jnp
from jax import lax
from jax.sharding import PartitionSpec as P

D = 1024
HEADS = 16
HD = 64
P_SIZE = 128
SEQ = 128


def norm_rows(values, scaling):
    average = jnp.mean(values, axis=-1, keepdims=True)
    centred = values - average
    variance = jnp.mean(centred * centred, axis=-1, keepdims=True)
    return centred * lax.rsqrt(variance + 1e-05) * scaling


def best_match(piece, flat_docs, live_doc):
    sims = lax.dot_general(
        piece, flat_docs, (((1,), (1,)), ((), ())), preferred_element_type=jnp.float32
    )
    sims = sims.reshape(piece.shape[0], live_doc.shape[0], live_doc.shape[1])
    sims = jnp.where(live_doc[None], sims, -1e30)
    return jnp.max(sims, axis=2)


def on_device(
    tokens,
    attend_weight,
    output_weight,
    attend_gain,
    up_weight,
    down_weight,
    mlp_gain,
    embed_weight,
    query_length,
    documents,
    document_length,
    candidates,
):
    rows = tokens.shape[0]
    requests = query_length.shape[0]
    held_docs = documents.shape[0]
    packed = jnp.dot(tokens, attend_weight, preferred_element_type=jnp.float32).astype(jnp.bfloat16)
    packed = packed.reshape(requests, SEQ, 3, HEADS, HD)
    live_slot = jnp.arange(SEQ)[None, :] < query_length[:, None]
    logits = jnp.einsum(
        "rqhd,rkhd->rhqk", packed[:, :, 0], packed[:, :, 1], preferred_element_type=jnp.float32
    ) * HD ** (-0.5)
    logits = jnp.where(live_slot[:, None, None, :], logits, -1e30)
    highest = jnp.max(logits, axis=-1, keepdims=True)
    weights = jnp.exp(logits - highest)
    probs = (weights / jnp.sum(weights, axis=-1, keepdims=True)).astype(jnp.bfloat16)
    context = jnp.einsum(
        "rhqk,rkhd->rqhd", probs, packed[:, :, 2], preferred_element_type=jnp.float32
    )
    context = context.astype(jnp.bfloat16).reshape(rows, D)
    attended = jnp.dot(context, output_weight, preferred_element_type=jnp.float32)
    normed = norm_rows(tokens.astype(jnp.float32) + attended, attend_gain).astype(jnp.bfloat16)
    hidden = jax.nn.gelu(
        jnp.dot(
            normed,
            lax.all_gather(up_weight, "mlp", axis=1, tiled=True),
            preferred_element_type=jnp.float32,
        ),
        approximate=False,
    ).astype(jnp.bfloat16)
    reduced = lax.dot_general(
        hidden,
        lax.all_gather(down_weight, "mlp", axis=1, tiled=True),
        (((1,), (1,)), ((), ())),
        preferred_element_type=jnp.float32,
    )
    layer_out = norm_rows(normed.astype(jnp.float32) + reduced, mlp_gain).astype(jnp.bfloat16)
    projected = jnp.dot(layer_out, embed_weight, preferred_element_type=jnp.float32)
    unit = projected * lax.rsqrt(jnp.sum(projected * projected, axis=-1, keepdims=True) + 1e-06)
    embedded = jnp.where(live_slot.reshape(rows, 1), unit, 0.0).astype(jnp.bfloat16)
    shard_rows = documents.shape[1]
    positions = lax.axis_index("mlp") * shard_rows + jnp.arange(shard_rows)
    live_doc = positions[None, :] < document_length[:, None]
    flat_docs = documents.reshape(held_docs * shard_rows, P_SIZE)
    partial_best = best_match(
        lax.all_gather(embedded, ("req", "mlp"), axis=0, tiled=True), flat_docs, live_doc
    )
    best = lax.pmax(partial_best.astype(jnp.bfloat16), "mlp").astype(partial_best.dtype)
    totals = jnp.sum(best.reshape(best.shape[0] // SEQ, SEQ, held_docs), axis=1)
    swapped = lax.all_to_all(totals, "req", split_axis=0, concat_axis=1, tiled=True)
    swapped = lax.dynamic_slice_in_dim(swapped, lax.axis_index("mlp") * requests, requests, 0)
    all_docs = swapped.shape[1]
    matches = candidates[:, :, None] == jnp.arange(all_docs, dtype=jnp.int32)[None, None, :]
    scores = jnp.sum(jnp.where(matches, swapped[:, None, :], 0.0), axis=2)
    return (embedded, scores)


def solution(mesh):
    return jax.shard_map(
        on_device,
        mesh=mesh,
        in_specs=(
            P(("req", "mlp"), None),
            P(),
            P(),
            P(),
            P(None, "mlp"),
            P(None, "mlp"),
            P(),
            P(),
            P(("req", "mlp")),
            P("req", "mlp", None),
            P("req"),
            P(("req", "mlp"), None),
        ),
        out_specs=(P(("req", "mlp"), None), P(("req", "mlp"), None)),
        check_vma=False,
    )
```

profile of v0, /device:TPU:0, one launch (start us, length us, event | category | flops | bytes accessed | tf_op | source)
XLA Modules:
  0.0 354.3 jit_solution(13701282405548366960)
XLA Ops:
  7.2 0.0 copy-start
  7.2 0.0 all-gather.4.cloned.1.call-start
  7.2 0.7 all-gather.4.cloned.1.call-update
  7.9 0.0 all-gather.6.cloned.1.call-start
  8.0 0.7 all-gather.6.cloned.1.call-update
  8.7 0.0 all-gather.8.cloned.1.call-start
  8.7 8.2 %convolution_convert_fusion = bf16[512,3072]{1,0:T(8,128)(2,1)} fusion(bf16[512,1024]{1,0:T(8,128)(2,1)} %param.12, bf16[1024,3072]{1,0:T(8,128)(2,1)} %param.13), kind=kOutput, calls=%fused_computation.23 | convolution fusion | flops 3222798336 | bytes 10485760 | tf_op jit(solution)/shard_map/dot_general | solution.py:46
  17.0 8.8 %reshape.125 = bf16[4,128,3,16,64]{4,3,2,1,0:T(8,128)(2,1)} reshape(bf16[512,3072]{1,0:T(8,128)(2,1)} %convolution_convert_fusion) | data formatting | bytes 6291456 | tf_op jit(solution)/shard_map/reshape | solution.py:47
  25.7 6.1 %fusion.70 = (bf16[4,128,1,16,64]{4,3,2,1,0:T(8,128)(2,1)}, bf16[4,128,1,16,64]{4,3,2,1,0:T(8,128)(2,1)}, bf16[4,128,1,16,64]{4,3,2,1,0:T(8,128)(2,1)}) fusion(bf16[4,128,3,16,64]{4,3,2,1,0:T(8,128)(2,1)} %reshape.125), kind=kLoop, calls=%fused_computation.100 | loop fusion | bytes 6291456 | tf_op jit(solution)/shard_map/slice | solution.py:57
  31.8 2.8 copy.70
  34.7 3.5 %copy.71 = bf16[4,128,1,16,64]{1,4,3,0,2:T(8,128)(2,1)} copy(bf16[4,128,1,16,64]{4,3,2,1,0:T(8,128)(2,1)} %get-tuple-element.14) | data formatting | bytes 2097152
  38.2 3.7 %copy.69 = bf16[4,128,1,16,64]{1,4,3,0,2:T(8,128)(2,1)} copy(bf16[4,128,1,16,64]{4,3,2,1,0:T(8,128)(2,1)} %get-tuple-element.12) | data formatting | bytes 2097152
  41.9 0.1 fusion.68
  42.0 2.1 fusion.29
  44.1 1.7 fusion.71
  45.8 0.0 copy-start.5
  45.8 0.7 fusion.25
  46.5 0.0 copy-start.11
  46.5 0.9 copy.56
  47.4 1.4 fusion.72
  48.8 1.3 copy-done.2
  50.2 0.3 multiply_reduce_fusion.1
  50.5 0.0 copy-start.9
  50.6 11.3 %all-gather.4.cloned.1.call-done = bf16[1024,4096]{1,0:T(8,128)(2,1)} async-done(((bf16[1024,512]{1,0:T(8,128)(2,1)}), bf16[1024,4096]{1,0:T(8,128)(2,1)}) %all-gather.4.cloned.1.call-update) | async-done | bytes 8388624 | tf_op jit(solution)/shard_map/all_gather | solution.py:65
  61.9 51.6 %all-gather.6.cloned.1.call-done = bf16[1024,4096]{1,0:T(8,128)(2,1)} async-done(((bf16[1024,512]{1,0:T(8,128)(2,1)}), bf16[1024,4096]{1,0:T(8,128)(2,1)}) %all-gather.6.cloned.1.call-update) | async-done | bytes 8388624 | tf_op jit(solution)/shard_map/all_gather | solution.py:72
  113.5 32.1 %fusion.73 = (f32[512]{0:T(512)S(1)}, f32[512,1024]{1,0:T(8,128)S(1)}) fusion(bf16[1024,4096]{1,0:T(8,128)(2,1)} %all-gather.6.cloned.1.call-done, f32[1024]{0:T(1024)S(1)} %copy-done.11, f32[512]{0:T(512)S(1)} %add_rsqrt_fusion.2, f32[512,1024]{1,0:T(8,128)} %copy-done.2, f32[512]{0:T(512)S(1)} %broadcast_multiply_fusion.1, ...), kind=kOutput, calls=%fused_computation.103 | convolution fusion | flops 8732016640 | bytes 20981760 | tf_op jit(solution)/shard_map/dot_general | solution.py:70
  145.7 0.3 multiply_reduce_fusion
  146.0 0.7 multiply_reduce_fusion.2
  146.7 0.7 select_convert_fusion
  147.4 0.0 all-gather.8.cloned.1.call-update
  147.4 0.0 all-reduce.2.cloned.1.call-start
  147.5 0.1 broadcast_compare_fusion
  147.6 91.0 %all-gather.8.cloned.1.call-done = bf16[65536,128]{0,1:T(8,128)(2,1)} async-done(((bf16[512,128]{0,1:T(8,128)(2,1)}), bf16[65536,128]{0,1:T(8,128)(2,1)}) %all-gather.8.cloned.1.call-update) | async-done | bytes 16777232 | tf_op jit(solution)/shard_map/all_gather | solution.py:85
  238.6 27.4 %fusion.2 = bf16[65536,8]{0,1:T(8,128)(2,1)} fusion(bf16[8,32,128]{2,1,0:T(8,128)(2,1)S(1)} %copy-done.10, bf16[65536,128]{0,1:T(8,128)(2,1)} %all-gather.8.cloned.1.call-done, pred[8,32]{1,0:T(8,128)(4,1)S(1)} %broadcast_compare_fusion), kind=kOutput, calls=%fused_computation.4 | convolution fusion | flops 4327997440 | bytes 17891584 | tf_op jit(solution)/shard_map/dot_general | solution.py:21
  266.0 0.0 all-reduce.2.cloned.1.call-update
  266.0 62.4 %all-reduce.2.cloned.1.call-done = bf16[512,128,8]{1,2,0:T(8,128)(2,1)} async-done(((bf16[512,128,8]{1,2,0:T(8,128)(2,1)}), bf16[512,128,8]{1,2,0:T(8,128)(2,1)}) %all-reduce.2.cloned.1.call-update) | async-done | bytes 1048592 | tf_op jit(solution)/shard_map/pmax | solution.py:87
  328.4 1.8 convert_reduce_fusion
  330.2 0.1 copy.59
  330.3 0.7 reshape.127
  331.1 6.9 %all-to-all-start = ((f32[16,1,256]{2,1,0:T(1,128)}), f32[16,1,256]{2,1,0:T(1,128)S(1)}, u32[]{:S(2)}, u32[]{:S(2)}) async-start(f32[16,1,256]{2,1,0:T(1,128)} %reshape.127), calls=%async_computation | async-start | bytes 32768 | tf_op jit(solution)/shard_map/all_to_all | solution.py:89
  338.0 0.8 copy.61
  338.8 6.8 %all-to-all-done = f32[16,1,256]{2,1,0:T(1,128)S(1)} async-done(((f32[16,1,256]{2,1,0:T(1,128)}), f32[16,1,256]{2,1,0:T(1,128)S(1)}, u32[]{:S(2)}, u32[]{:S(2)}) %all-to-all-start) | async-done | bytes 16416 | tf_op jit(solution)/shard_map/all_to_all | solution.py:89
  345.6 0.5 broadcast.105
  346.1 0.7 reduce
  346.8 0.1 reshape.128
  346.9 0.1 constant_dynamic-slice_fusion
  347.0 0.1 copy.60
  347.0 0.8 select_reduce_fusion
  (28 shorter events, 0.1 us)
Async XLA Ops:
  7.2 40.2 %copy-start = (bf16[1024,1024]{1,0:T(8,128)(2,1)S(1)}, bf16[1024,1024]{1,0:T(8,128)(2,1)}, u32[]{:S(2)}) copy-start(bf16[1024,1024]{1,0:T(8,128)(2,1)} %param.14) | copy-start | bytes 6291460
  7.2 54.7 %all-gather.4.cloned.1.call-start = ((), (), s32[]{:S(2)}) async-start(), calls=%async_computation.1 | async-start | bytes 9437184 | tf_op jit(solution)/shard_map/all_gather | solution.py:65
  7.9 105.6 %all-gather.6.cloned.1.call-start = ((), (), s32[]{:S(2)}) async-start(), calls=%async_computation.2 | async-start | bytes 9437184 | tf_op jit(solution)/shard_map/all_gather | solution.py:72
  8.7 229.9 %all-gather.8.cloned.1.call-start = ((), (), s32[]{:S(2)}) async-start(), calls=%async_computation.3 | async-start | bytes 16908288 | tf_op jit(solution)/shard_map/all_gather | solution.py:85
  25.7 16.2 %copy-start.12 = (s32[4]{0:T(128)S(1)}, s32[4]{0:T(128)}, u32[]{:S(2)}) copy-start(s32[4]{0:T(128)} %param.20) | copy-start | bytes 52
  41.9 3.9 %copy-start.4 = (bf16[4,128,1,16,64]{1,4,3,0,2:T(8,128)(2,1)S(1)}, bf16[4,128,1,16,64]{1,4,3,0,2:T(8,128)(2,1)}, u32[]{:S(2)}) copy-start(bf16[4,128,1,16,64]{1,4,3,0,2:T(8,128)(2,1)} %copy.69) | copy-start | bytes 3145732
  45.8 1.7 copy-start.5
  46.5 67.0 %copy-start.11 = (f32[1024]{0:T(1024)S(1)}, f32[1024]{0:T(1024)}, u32[]{:S(2)}) copy-start(f32[1024]{0:T(1024)} %param.15) | copy-start | bytes 12292
  48.8 1.4 copy-start.2
  50.5 95.5 %copy-start.6 = (bf16[1024,128]{1,0:T(8,128)(2,1)S(1)}, bf16[1024,128]{1,0:T(8,128)(2,1)}, u32[]{:S(2)}) copy-start(bf16[1024,128]{1,0:T(8,128)(2,1)} %param.19) | copy-start | bytes 786436
  50.5 95.5 %copy-start.7 = (f32[1024]{0:T(1024)S(1)}, f32[1024]{0:T(1024)}, u32[]{:S(2)}) copy-start(f32[1024]{0:T(1024)} %param.18) | copy-start | bytes 12292
  50.5 97.0 %copy-start.9 = (s32[8]{0:T(128)S(1)}, s32[8]{0:T(128)}, u32[]{:S(2)}) copy-start(s32[8]{0:T(128)} %param.22) | copy-start | bytes 100
  50.5 188.0 %copy-start.10 = (bf16[8,32,128]{2,1,0:T(8,128)(2,1)S(1)}, bf16[8,32,128]{2,1,0:T(8,128)(2,1)}, u32[]{:S(2)}) copy-start(bf16[8,32,128]{2,1,0:T(8,128)(2,1)} %param.21) | copy-start | bytes 196612
  147.4 180.9 %all-reduce.2.cloned.1.call-start = ((), (), s32[]{:S(2)}) async-start(), calls=%async_computation.4 | async-start | bytes 2097152 | tf_op jit(solution)/shard_map/pmax | solution.py:87
  147.6 190.4 %copy-start.3 = (bf16[512,128]{0,1:T(8,128)(2,1)S(1)}, bf16[512,128]{0,1:T(8,128)(2,1)}, u32[]{:S(2)}) copy-start(bf16[512,128]{0,1:T(8,128)(2,1)} %select_convert_fusion) | copy-start | bytes 393220
  147.6 199.5 %copy-start.8 = (s32[4,8]{1,0:T(4,128)S(1)}, s32[4,8]{1,0:T(4,128)}, u32[]{:S(2)}) copy-start(s32[4,8]{1,0:T(4,128)} %param.23) | copy-start | bytes 388
  238.6 109.2 %copy-start.1 = (bf16[1024,1024]{1,0:T(8,128)(2,1)S(1)}, bf16[1024,1024]{1,0:T(8,128)(2,1)}, u32[]{:S(2)}) copy-start(bf16[1024,1024]{1,0:T(8,128)(2,1)} %param.14) | copy-start | bytes 6291460
  331.1 14.5 %all-to-all-start = ((f32[16,1,256]{2,1,0:T(1,128)}), f32[16,1,256]{2,1,0:T(1,128)S(1)}, u32[]{:S(2)}, u32[]{:S(2)}) async-start(f32[16,1,256]{2,1,0:T(1,128)} %reshape.127), calls=%async_computation | async-start | bytes 32768 | tf_op jit(solution)/shard_map/all_to_all | solution.py:89
Sparse Core Ops, SparseCore 0:
  9.7 52.1 all-gather.3
  63.6 49.8 all-gather.5
  147.5 90.9 all-gather.7
  266.1 62.1 all-reduce.1
where the time goes:
time: 355 us; the launch traced here: 354 us
  waiting for transfers between devices  225 us (63%)
  matrix products  72.6 us (20%)
  local copies, waits for them, and re-layouts  29.5 us (8%)
  between operations  14 us (4%)
  starting transfers between devices  7.1 us (2%)
  other arithmetic  6.53 us (2%)
    all_gather x1, waiting for transfers between devices, on_device(): lax.all_gather(embedded, ('req', 'mlp'), axis=0, tiled=True)  91 us
    pmax x1, waiting for transfers between devices, on_device(): lax.pmax(partial_best.astype(jnp.bfloat16), 'mlp')  62.4 us
    all_gather x1, waiting for transfers between devices, on_device(): lax.all_gather(down_weight, 'mlp', axis=1, tiled=True)  51.6 us
    dot_general x1, matrix products, on_device(): lax.dot_general(hidden, lax.all_gather(down_weight, 'mlp', axis=1, tiled=...  32.1 us
    dot_general x1, matrix products, best_match(): lax.dot_general(piece, flat_docs, (((1,), (1,)), ((), ())), preferred_ele...  27.4 us
    unnamed x32, local copies, waits for them, and re-layouts  13 us
    all_gather x1, waiting for transfers between devices, on_device(): lax.all_gather(up_weight, 'mlp', axis=1, tiled=True)  11.3 us
    reshape x1, local copies, waits for them, and re-layouts, on_device(): packed = packed.reshape(requests, SEQ, 3, HEADS, HD)  8.77 us
  transfers between devices with their start and end apart: 5, of which 5 were waited for; matrix products, arithmetic and copies ran while one was open for 12% of the time, Pallas kernels for 0%

commit v1 on v0

--- a/solution.py
+++ b/solution.py
@@ -8,6 +8,18 @@
 HD = 64
 P_SIZE = 128
 SEQ = 128
+
+
+def supply_all_members_all(packet):
+    return jnp.concatenate(
+        lax.all_to_all(
+            jnp.stack(tuple((packet for _ in range(lax.psum(1, axis_name="mlp"))))),
+            split_axis=0,
+            axis_name="mlp",
+            concat_axis=0,
+        ),
+        axis=1,
+    )
 
 
 def norm_rows(values, scaling):
@@ -69,7 +81,7 @@
     ).astype(jnp.bfloat16)
     reduced = lax.dot_general(
         hidden,
-        lax.all_gather(down_weight, "mlp", axis=1, tiled=True),
+        supply_all_members_all(down_weight),
         (((1,), (1,)), ((), ())),
         preferred_element_type=jnp.float32,
     )

time: 355 us -> 389 us (1.096)
  waiting for transfers between devices: 225 us -> 248 us
  local copies, waits for them, and re-layouts: 29.5 us -> 35.1 us
  starting transfers between devices: 7.1 us -> 12.2 us
    all_to_all x0 -> x1, waiting for transfers between devices: none -> 87.1 us  [supply_all_members_all(): lax.all_to_all(jnp.stack(tuple((packet for _ in range(lax.psum(1, axis_na...]
    all_gather x1 -> x0, waiting for transfers between devices: 51.6 us -> none  [on_device(): lax.all_gather(down_weight, 'mlp', axis=1, tiled=True)]
    all_gather x1, waiting for transfers between devices: 11.3 us -> 0.01 us  [on_device(): lax.all_gather(up_weight, 'mlp', axis=1, tiled=True)]
    all_to_all x0 -> x1, starting transfers between devices: none -> 5.17 us  [supply_all_members_all(): lax.all_to_all(jnp.stack(tuple((packet for _ in range(lax.psum(1, axis_na...]
    another operation x0 -> x1, local copies, waits for them, and re-layouts: none -> 4.31 us  [supply_all_members_all(): jnp.stack(tuple((packet for _ in range(lax.psum(1, axis_name='mlp')))))]
    unnamed x32 -> x35, local copies, waits for them, and re-layouts: 13 us -> 14.4 us
  transfers between devices with their start and end apart: 5 -> 5, of which waited for: 5 -> 4; matrix products, arithmetic and copies ran while one was open for 12% -> 12% of each run, Pallas kernels for 0% -> 0%
where the time goes in v1:
time: 389 us
  waiting for transfers between devices  248 us (64%)
  matrix products  72.5 us (19%)
  local copies, waits for them, and re-layouts  35.1 us (9%)
  between operations  14 us (4%)
  starting transfers between devices  12.2 us (3%)
  other arithmetic  6.53 us (2%)
    all_gather x1, waiting for transfers between devices, on_device(): lax.all_gather(embedded, ('req', 'mlp'), axis=0, tiled=True)  91.3 us
    all_to_all x1, waiting for transfers between devices, supply_all_members_all(): lax.all_to_all(jnp.stack(tuple((packet for _ in range(lax.psum(1, axis_na...  87.1 us
    pmax x1, waiting for transfers between devices, on_device(): lax.pmax(partial_best.astype(jnp.bfloat16), 'mlp')  62.4 us
    dot_general x1, matrix products, on_device(): lax.dot_general(hidden, supply_all_members_all(down_weight), (((1,), (1,)...  32.4 us
    dot_general x1, matrix products, best_match(): lax.dot_general(piece, flat_docs, (((1,), (1,)), ((), ())), preferred_ele...  27.4 us
    unnamed x35, local copies, waits for them, and re-layouts  14.4 us
    reshape x1, local copies, waits for them, and re-layouts, on_device(): packed = packed.reshape(requests, SEQ, 3, HEADS, HD)  8.61 us
    dot_general x1, matrix products, on_device(): jnp.dot(tokens, attend_weight, preferred_element_type=jnp.float32)  7.86 us
  transfers between devices with their start and end apart: 5, of which 4 were waited for; matrix products, arithmetic and copies ran while one was open for 12% of the time, Pallas kernels for 0%

profile of v1, /device:TPU:0, one launch (start us, length us, event | category | flops | bytes accessed | tf_op | source)
XLA Modules:
  0.0 388.6 jit_solution(17180622559967837678)
XLA Ops:
  7.2 0.0 copy-start
  7.2 0.0 all-gather.3.cloned.1.call-start
  7.2 0.7 all-gather.3.cloned.1.call-update
  7.9 1.5 copy.60
  9.4 4.3 %stack.2 = bf16[8,1024,512]{1,2,0:T(8,128)(2,1)} broadcast(bf16[1024,512]{0,1:T(8,128)(2,1)S(1)} %copy.60), dimensions={1,2} | broadcast | bytes 9437184 | tf_op jit(solution)/shard_map/stack | solution.py:16
  13.7 5.2 %all-to-all-start = ((bf16[8,1024,512]{1,2,0:T(8,128)(2,1)}), bf16[8,1024,512]{1,2,0:T(8,128)(2,1)}, u32[]{:S(2)}, u32[]{:S(2)}) async-start(bf16[8,1024,512]{1,2,0:T(8,128)(2,1)} %stack.2), calls=%async_computation | async-start | bytes 16777216 | tf_op jit(solution)/shard_map/all_to_all | solution.py:15
  18.9 0.0 all-gather.5.cloned.1.call-start
  19.0 7.9 %convolution_convert_fusion = bf16[512,3072]{1,0:T(8,128)(2,1)} fusion(bf16[512,1024]{1,0:T(8,128)(2,1)S(1)} %copy-done.5, bf16[1024,3072]{1,0:T(8,128)(2,1)} %param.13), kind=kOutput, calls=%fused_computation.23 | convolution fusion | flops 3222798336 | bytes 10485760 | tf_op jit(solution)/shard_map/dot_general | solution.py:58
  26.8 8.6 %reshape.135 = bf16[4,128,3,16,64]{4,3,2,1,0:T(8,128)(2,1)} reshape(bf16[512,3072]{1,0:T(8,128)(2,1)} %convolution_convert_fusion) | data formatting | bytes 6291456 | tf_op jit(solution)/shard_map/reshape | solution.py:59
  35.4 6.0 %fusion.70 = (bf16[4,128,1,16,64]{4,3,2,1,0:T(8,128)(2,1)}, bf16[4,128,1,16,64]{4,3,2,1,0:T(8,128)(2,1)}, bf16[4,128,1,16,64]{4,3,2,1,0:T(8,128)(2,1)}) fusion(bf16[4,128,3,16,64]{4,3,2,1,0:T(8,128)(2,1)} %reshape.135), kind=kLoop, calls=%fused_computation.100 | loop fusion | bytes 6291456 | tf_op jit(solution)/shard_map/slice | solution.py:69
  41.5 2.8 copy.74
  44.3 3.6 copy.75
  47.9 3.5 copy.73
  51.4 0.1 fusion.68
  51.5 2.1 fusion.29
  53.6 1.7 fusion.71
  55.3 0.0 copy-start.6
  55.3 0.7 fusion.25
  56.0 0.0 copy-start.12
  56.0 0.9 copy.59
  57.0 1.4 fusion.72
  58.4 1.4 copy-done.2
  59.7 0.3 multiply_reduce_fusion.1
  60.1 87.1 %all-to-all-done = bf16[8,1024,512]{1,2,0:T(8,128)(2,1)} async-done(((bf16[8,1024,512]{1,2,0:T(8,128)(2,1)}), bf16[8,1024,512]{1,2,0:T(8,128)(2,1)}, u32[]{:S(2)}, u32[]{:S(2)}) %all-to-all-start) | async-done | bytes 8388640 | tf_op jit(solution)/shard_map/all_to_all | solution.py:15
  147.2 0.0 copy-start.10
  147.3 32.4 %fusion.73 = (f32[512]{0:T(512)S(1)}, f32[512,1024]{1,0:T(8,128)S(1)}) fusion(bf16[1024,4096]{0,1:T(8,128)(2,1)} %bitcast.6, f32[1024]{0:T(1024)S(1)} %copy-done.12, f32[512]{0:T(512)S(1)} %add_rsqrt_fusion.2, f32[512,1024]{1,0:T(8,128)} %copy-done.2, f32[512]{0:T(512)S(1)} %broadcast_multiply_fusion.1, bf16[1024,4096]{1,0:T(8,128)(2,1)} %all-gather.3.cloned.1.call-done), kind=kOutput, calls=%fused_computation.103 | convolution fusion | flops 8732016640 | bytes 20981760 | tf_op jit(solution)/shard_map/dot_general | solution.py:82
  179.7 0.3 multiply_reduce_fusion
  180.0 0.7 multiply_reduce_fusion.2
  180.7 0.7 select_convert_fusion
  181.4 0.0 all-gather.5.cloned.1.call-update
  181.4 0.0 all-reduce.2.cloned.1.call-start
  181.5 0.1 broadcast_compare_fusion
  181.6 91.3 %all-gather.5.cloned.1.call-done = bf16[65536,128]{0,1:T(8,128)(2,1)} async-done(((bf16[512,128]{0,1:T(8,128)(2,1)}), bf16[65536,128]{0,1:T(8,128)(2,1)}) %all-gather.5.cloned.1.call-update) | async-done | bytes 16777232 | tf_op jit(solution)/shard_map/all_gather | solution.py:97
  272.8 27.4 %fusion.2 = bf16[65536,8]{0,1:T(8,128)(2,1)} fusion(bf16[8,32,128]{2,1,0:T(8,128)(2,1)S(1)} %copy-done.11, bf16[65536,128]{0,1:T(8,128)(2,1)} %all-gather.5.cloned.1.call-done, pred[8,32]{1,0:T(8,128)(4,1)S(1)} %broadcast_compare_fusion), kind=kOutput, calls=%fused_computation.4 | convolution fusion | flops 4327997440 | bytes 17891584 | tf_op jit(solution)/shard_map/dot_general | solution.py:33
  300.3 0.0 all-reduce.2.cloned.1.call-update
  300.3 62.4 %all-reduce.2.cloned.1.call-done = bf16[512,128,8]{1,2,0:T(8,128)(2,1)} async-done(((bf16[512,128,8]{1,2,0:T(8,128)(2,1)}), bf16[512,128,8]{1,2,0:T(8,128)(2,1)}) %all-reduce.2.cloned.1.call-update) | async-done | bytes 1048592 | tf_op jit(solution)/shard_map/pmax | solution.py:99
  362.6 1.8 convert_reduce_fusion
  364.5 0.1 copy.63
  364.6 0.7 reshape.137
  365.3 6.9 %all-to-all-start.1 = ((f32[16,1,256]{2,1,0:T(1,128)}), f32[16,1,256]{2,1,0:T(1,128)S(1)}, u32[]{:S(2)}, u32[]{:S(2)}) async-start(f32[16,1,256]{2,1,0:T(1,128)} %reshape.137), calls=%async_computation.1 | async-start | bytes 32768 | tf_op jit(solution)/shard_map/all_to_all | solution.py:101
  372.3 0.8 copy.65
  373.0 6.8 %all-to-all-done.1 = f32[16,1,256]{2,1,0:T(1,128)S(1)} async-done(((f32[16,1,256]{2,1,0:T(1,128)}), f32[16,1,256]{2,1,0:T(1,128)S(1)}, u32[]{:S(2)}, u32[]{:S(2)}) %all-to-all-start.1) | async-done | bytes 16416 | tf_op jit(solution)/shard_map/all_to_all | solution.py:101
  379.9 0.5 broadcast.107
  380.4 0.7 reduce
  381.1 0.1 reshape.138
  381.1 0.1 constant_dynamic-slice_fusion
  381.2 0.1 copy.64
  381.3 0.8 select_reduce_fusion
  (31 shorter events, 0.1 us)
Async XLA Ops:
  7.2 49.8 %copy-start = (bf16[1024,1024]{1,0:T(8,128)(2,1)S(1)}, bf16[1024,1024]{1,0:T(8,128)(2,1)}, u32[]{:S(2)}) copy-start(bf16[1024,1024]{1,0:T(8,128)(2,1)} %param.14) | copy-start | bytes 6291460
  7.2 140.0 %all-gather.3.cloned.1.call-start = ((), (), s32[]{:S(2)}) async-start(), calls=%async_computation.2 | async-start | bytes 9437184 | tf_op jit(solution)/shard_map/all_gather | solution.py:77
  13.7 5.2 %copy-start.5 = (bf16[512,1024]{1,0:T(8,128)(2,1)S(1)}, bf16[512,1024]{1,0:T(8,128)(2,1)}, u32[]{:S(2)}) copy-start(bf16[512,1024]{1,0:T(8,128)(2,1)} %param.12) | copy-start | bytes 3145732
  13.7 133.5 %all-to-all-start = ((bf16[8,1024,512]{1,2,0:T(8,128)(2,1)}), bf16[8,1024,512]{1,2,0:T(8,128)(2,1)}, u32[]{:S(2)}, u32[]{:S(2)}) async-start(bf16[8,1024,512]{1,2,0:T(8,128)(2,1)} %stack.2), calls=%async_computation | async-start | bytes 16777216 | tf_op jit(solution)/shard_map/all_to_all | solution.py:15
  18.9 253.9 %all-gather.5.cloned.1.call-start = ((), (), s32[]{:S(2)}) async-start(), calls=%async_computation.3 | async-start | bytes 16908288 | tf_op jit(solution)/shard_map/all_gather | solution.py:97
  35.4 16.0 %copy-start.13 = (s32[4]{0:T(128)S(1)}, s32[4]{0:T(128)}, u32[]{:S(2)}) copy-start(s32[4]{0:T(128)} %param.20) | copy-start | bytes 52
  51.4 3.8 copy-start.4
  55.3 1.7 copy-start.6
  56.0 91.2 %copy-start.12 = (f32[1024]{0:T(1024)S(1)}, f32[1024]{0:T(1024)}, u32[]{:S(2)}) copy-start(f32[1024]{0:T(1024)} %param.15) | copy-start | bytes 12292
  58.3 1.4 copy-start.2
  147.2 32.8 %copy-start.7 = (bf16[1024,128]{1,0:T(8,128)(2,1)S(1)}, bf16[1024,128]{1,0:T(8,128)(2,1)}, u32[]{:S(2)}) copy-start(bf16[1024,128]{1,0:T(8,128)(2,1)} %param.19) | copy-start | bytes 786436
  147.2 32.8 %copy-start.8 = (f32[1024]{0:T(1024)S(1)}, f32[1024]{0:T(1024)}, u32[]{:S(2)}) copy-start(f32[1024]{0:T(1024)} %param.18) | copy-start | bytes 12292
  147.2 34.3 %copy-start.10 = (s32[8]{0:T(128)S(1)}, s32[8]{0:T(128)}, u32[]{:S(2)}) copy-start(s32[8]{0:T(128)} %param.22) | copy-start | bytes 100
  147.2 125.6 %copy-start.11 = (bf16[8,32,128]{2,1,0:T(8,128)(2,1)S(1)}, bf16[8,32,128]{2,1,0:T(8,128)(2,1)}, u32[]{:S(2)}) copy-start(bf16[8,32,128]{2,1,0:T(8,128)(2,1)} %param.21) | copy-start | bytes 196612
  181.4 181.2 %all-reduce.2.cloned.1.call-start = ((), (), s32[]{:S(2)}) async-start(), calls=%async_computation.4 | async-start | bytes 2097152 | tf_op jit(solution)/shard_map/pmax | solution.py:99
  181.6 190.7 %copy-start.3 = (bf16[512,128]{0,1:T(8,128)(2,1)S(1)}, bf16[512,128]{0,1:T(8,128)(2,1)}, u32[]{:S(2)}) copy-start(bf16[512,128]{0,1:T(8,128)(2,1)} %select_convert_fusion) | copy-start | bytes 393220
  181.6 199.7 %copy-start.9 = (s32[4,8]{1,0:T(4,128)S(1)}, s32[4,8]{1,0:T(4,128)}, u32[]{:S(2)}) copy-start(s32[4,8]{1,0:T(4,128)} %param.23) | copy-start | bytes 388
  272.8 109.2 %copy-start.1 = (bf16[1024,1024]{1,0:T(8,128)(2,1)S(1)}, bf16[1024,1024]{1,0:T(8,128)(2,1)}, u32[]{:S(2)}) copy-start(bf16[1024,1024]{1,0:T(8,128)(2,1)} %param.14) | copy-start | bytes 6291460
  365.3 14.5 %all-to-all-start.1 = ((f32[16,1,256]{2,1,0:T(1,128)}), f32[16,1,256]{2,1,0:T(1,128)S(1)}, u32[]{:S(2)}, u32[]{:S(2)}) async-start(f32[16,1,256]{2,1,0:T(1,128)} %reshape.137), calls=%async_computation.1 | async-start | bytes 32768 | tf_op jit(solution)/shard_map/all_to_all | solution.py:101
Sparse Core Ops, SparseCore 0:
  9.7 96.4 all-gather.2
  181.5 91.2 all-gather.4
  300.4 62.1 all-reduce.1
